TPU v7x, 32 devices: a whole 2x2x4 slice. The times are simulated.
32 devices in a mesh: groups: 1, ep: 32 (over z, y, x, core).
Axes of the slice: x: 2, y: 2, z: 4, core: 2. Of those that a mesh axis runs over, the one named last changes fastest.
Arguments:
- tokens: bfloat16 [256, 7168], P(('groups', 'ep')), may hold values from -6 to 6
- expert_ids: int32 [256, 2], P(('groups', 'ep')), may hold values from 0 to 3, all different within a row; in each aligned block of 8 rows (0 to 7, 8 to 15, ...) at most 8 rows name the same one
- affinity: float32 [256, 2], P(('groups', 'ep')), may hold values from 0.05 to 1
- w_gate: bfloat16 [32, 7168, 256], P('ep'), may hold values from -0.0625 to 0.0625
- w_up: bfloat16 [32, 7168, 256], P('ep'), may hold values from -0.0625 to 0.0625
- w_down: bfloat16 [32, 256, 7168], P('ep'), may hold values from -0.125 to 0.125
Outputs:
- moe_out: bfloat16 [256, 7168], P(('groups', 'ep'))
Inputs may be any that keep to these rules, and one draw needn't show every extreme that they name: `expert_ids`: each token names 2 different experts. Among the 8 tokens of one device no expert is named more than 8 times, and in every draw some device names some expert exactly 8 times.
All inputs are finite; a program needn't handle non-finite values.
Results may differ from a plain program's by a relative error of at most 0.008.
Values may be sent and summed in bfloat16 or wider, within the bound.
A program may use at most 128 MiB of HBM per device.

v0:
```python
import jax
import jax.numpy as jnp
from jax import lax
from jax.sharding import PartitionSpec as P

SPLIT = 8


route_scale = 2.5


def slots_of(expert_ids, experts):
    flat = expert_ids.reshape(-1)
    onehot = (flat[:, None] == jnp.arange(experts, dtype=jnp.int32)[None, :]).astype(jnp.int32)
    earlier = jnp.cumsum(onehot, axis=0) - onehot
    return jnp.sum(earlier * onehot, axis=1).reshape(expert_ids.shape)


def body(tokens, expert_ids, affinity, w_gate, w_up, w_down):
    devices = lax.axis_size("ep")
    experts = devices // SPLIT
    tok_rows = tokens.shape[0]
    routes = expert_ids.shape[1]
    width = tokens.shape[1]
    capacity = min(tok_rows, max(2, 2 * tok_rows * routes // experts))
    route_weight = route_scale * affinity / jnp.sum(affinity, axis=1, keepdims=True)
    slot = slots_of(expert_ids, experts)
    slot_key = expert_ids * capacity + slot
    columns = jnp.arange(experts * capacity, dtype=jnp.int32)
    matches = slot_key[:, :, None] == columns[None, None, :]
    select = jnp.sum(matches.astype(jnp.float32), axis=1).astype(jnp.bfloat16)
    outgoing = jnp.repeat(
        jnp.dot(select.T, tokens, preferred_element_type=jnp.float32)
        .astype(jnp.bfloat16)
        .reshape(experts, capacity, width),
        SPLIT,
        axis=0,
    )
    received = lax.all_to_all(outgoing, "ep", split_axis=0, concat_axis=0, tiled=True)
    rows = received.reshape(-1, width)
    gate = jnp.dot(rows, w_gate[0], preferred_element_type=jnp.float32)
    up = jnp.dot(rows, w_up[0], preferred_element_type=jnp.float32)
    hidden = (jax.nn.silu(gate) * up).astype(jnp.bfloat16)
    partial_value = jnp.dot(hidden, w_down[0], preferred_element_type=jnp.float32).astype(
        jnp.bfloat16
    )
    back = lax.all_to_all(
        partial_value.reshape(received.shape), "ep", split_axis=0, concat_axis=0, tiled=True
    )
    summed = jnp.sum(back.reshape(experts, SPLIT, capacity, width), axis=1, dtype=jnp.float32)
    combine = jnp.sum(jnp.where(matches, route_weight[:, :, None], 0.0), axis=1)
    mixed = jnp.dot(
        combine,
        summed.reshape(experts * capacity, width),
        precision=lax.Precision.HIGHEST,
        preferred_element_type=jnp.float32,
    )
    return mixed.astype(jnp.bfloat16)


def solution(mesh):
    return jax.shard_map(
        body,
        mesh=mesh,
        in_specs=(
            P(("groups", "ep"), None),
            P(("groups", "ep"), None),
            P(("groups", "ep"), None),
            P("ep", None, None),
            P("ep", None, None),
            P("ep", None, None),
        ),
        out_specs=P(("groups", "ep"), None),
        check_vma=False,
    )
```

profile of v0, /device:TPU:0, one launch (start us, length us, event | category | flops | bytes accessed | tf_op | source)
XLA Modules:
  0.0 194.5 jit_solution(15565348278835198464)
XLA Ops:
  0.0 0.0 copy-start
  0.0 0.7 reduce_sum.46
  0.7 0.7 multiply_divide_fusion
  1.4 0.8 copy.13
  2.2 0.1 eq.28
  2.3 0.1 fusion.30
  2.4 0.2 select_reduce_fusion.1
  2.6 0.1 reshape.25
  2.6 0.1 copy.15
  2.7 0.1 convert_reduce_fusion.1
  2.8 0.0 copy-done
  2.8 0.3 fusion.1
  3.1 0.4 broadcast_in_dim.22
  3.6 0.0 copy-start.2
  3.6 90.2 %all_to_all.10 = bf16[32,8,7168]{2,1,0:T(8,128)(2,1)S(1)} all-to-all(bf16[32,8,7168]{2,1,0:T(8,128)(2,1)S(1)} %bitcast.40), channel_id=1, replica_groups=mesh['groups'=1,'ep'=32] {'ep'}, dimensions={0} | all-to-all | bytes 7340032 | tf_op jit(solution)/shard_map/all_to_all | solution.py:39
  93.7 0.0 copy-start.1
  93.7 1.8 copy-done.1
  95.5 0.0 copy-done.2
  95.5 1.1 fusion.5
  96.6 10.0 %fusion = bf16[32,8,7168]{2,1,0:T(8,128)(2,1)} fusion(bf16[1,256,7168]{2,1,0:T(8,128)(2,1)} %param.11, bf16[1,7168,256]{2,1,0:T(8,128)(2,1)} %param.10, bf16[32,8,7168]{2,1,0:T(8,128)(2,1)} %copy-done.1, f32[256,256]{1,0:T(8,128)S(1)} %fusion.5), kind=kOutput, calls=%fused_computation.1 | convolution fusion | flops 1881276416 | bytes 14942208 | tf_op jit(solution)/shard_map/dot_general | solution.py:44
  106.7 86.1 %all_to_all.11 = bf16[32,8,7168]{2,1,0:T(8,128)(2,1)S(1)} all-to-all(bf16[32,8,7168]{2,1,0:T(8,128)(2,1)} %fusion), channel_id=1, replica_groups=mesh['groups'=1,'ep'=32] {'ep'}, dimensions={0} | all-to-all | bytes 7340032 | tf_op jit(solution)/shard_map/all_to_all | solution.py:47
  192.7 0.6 convert_reduce_fusion
  193.3 1.2 convolution_convert_fusion.2
  (2 shorter events, 0.0 us)
Async XLA Ops:
  0.0 2.8 %copy-start = (bf16[8,7168]{1,0:T(8,128)(2,1)S(1)}, bf16[8,7168]{1,0:T(8,128)(2,1)}, u32[]{:S(2)}) copy-start(bf16[8,7168]{1,0:T(8,128)(2,1)} %param.6) | copy-start | bytes 344068
  3.6 92.0 %copy-start.2 = (bf16[1,7168,256]{2,1,0:T(8,128)(2,1)S(1)}, bf16[1,7168,256]{2,1,0:T(8,128)(2,1)}, u32[]{:S(2)}) copy-start(bf16[1,7168,256]{2,1,0:T(8,128)(2,1)} %param.9) | copy-start | bytes 11010052
  93.7 1.8 copy-start.1
where the time goes:
time: 195 us; the launch traced here: 194 us
  blocking collectives  176 us (90%)
  matrix products  12.7 us (7%)
  local copies, waits for them, and re-layouts  3.21 us (2%)
  other arithmetic  2.36 us (1%)
    all_to_all x1, blocking collectives, body(): lax.all_to_all(outgoing, 'ep', split_axis=0, concat_axis=0, tiled=True)  90.2 us
    all_to_all x1, blocking collectives, body(): lax.all_to_all(partial_value.reshape(received.shape), 'ep', split_axis=0,...  86.1 us
    dot_general x1, matrix products, body(): jnp.dot(hidden, w_down[0], preferred_element_type=jnp.float32)  10 us

commit v1 on v0

v1 whole, which is shorter than its diff:
```python
import functools

import jax
import jax.numpy as jnp
from jax import lax
from jax.experimental import pallas as pl
from jax.experimental.pallas import tpu as pltpu
from jax.sharding import PartitionSpec as P

SPLIT = 8
CORES = 2
QUADS = SPLIT // CORES
MESH = pl.DeviceIdType.MESH
VMEM_LIMIT = 63 * 1024 * 1024

route_scale = 2.5


def tile_of(size, most):
    best = 128
    for tile in range(128, most + 1, 128):
        if size % tile == 0:
            best = tile
    return best


def kernel(
    experts,
    tok_hbm, ids_ref, aff_ref, gate_hbm, up_hbm, down_hbm,
    out_ref,
    tok, part, rb3, rb2, rb1, rb0, gate_w, up_w, down_w,
    load_sem, w_sem, tok_recv, z_send, s1_send, s2_send, s3_send,
    r3_recv, r3_send, r2_recv, r2_send, r1_recv, r1_send, r0_recv, r0_send,
):
    E = experts
    rows, width = tok_hbm.shape
    hid = gate_w.shape[1]
    me = lax.axis_index("ep")
    z = me // SPLIT
    j = me % SPLIT
    c = j % 2
    x = (j // 2) % 2
    y = j // 4
    dx = 2 * (1 - 2 * x)
    dy = 4 * (1 - 2 * y)
    ja = j + (1 - c) * dy + c * dx
    jb = j + c * dy + (1 - c) * dx
    jab = j + dx + dy
    js = j + 1 - 2 * c
    base = z * SPLIT
    dev_a, dev_b, dev_s = base + ja, base + jb, base + js

    def plane(k):
        return (z + k) % E

    loads = [
        pltpu.make_async_copy(tok_hbm, tok.at[me], load_sem),
        pltpu.make_async_copy(gate_hbm.at[0], gate_w, w_sem.at[0]),
        pltpu.make_async_copy(up_hbm.at[0], up_w, w_sem.at[1]),
        pltpu.make_async_copy(down_hbm.at[0], down_w, w_sem.at[2]),
    ]
    for load in loads:
        load.start()

    barrier = pltpu.get_barrier_semaphore()
    peers = [dev_a, dev_b, dev_s] + [((z + k) % E) * SPLIT + j for k in range(1, E)]
    for peer in peers:
        pl.semaphore_signal(barrier, inc=1, device_id={"ep": peer}, device_id_type=MESH)
    pl.semaphore_wait(barrier, len(peers))

    sends = []

    def send(src, dst, send_sem, recv_sem, device):
        copy = pltpu.make_async_remote_copy(
            src_ref=src, dst_ref=dst, send_sem=send_sem, recv_sem=recv_sem,
            device_id={"ep": device}, device_id_type=MESH,
        )
        copy.start()
        sends.append(copy)

    def arrived(dst, recv_sem):
        pltpu.make_async_remote_copy(
            src_ref=dst, dst_ref=dst, send_sem=load_sem, recv_sem=recv_sem,
            device_id={"ep": dev_s}, device_id_type=MESH,
        ).wait_recv()

    def tok_arrived(unit):
        arrived(tok.at[unit], tok_recv.at[unit])

    def pass_on(src, unit, sem, device):
        send(src, tok.at[unit], sem, tok_recv.at[unit], device)

    def own(k):
        return tok_hbm if k == 0 else tok.at[plane(k) * SPLIT + j]

    def f1(k):
        unit = plane(k) * SPLIT + j
        if k > 0:
            tok_arrived(unit)
        pass_on(own(k), unit, s1_send.at[k], dev_a)
        pass_on(own(k), unit, s3_send.at[k, 0], dev_s)

    def f2(k):
        unit, unit_a = plane(k) * SPLIT + j, plane(k) * SPLIT + ja
        pass_on(own(k), unit, s2_send.at[k, 0], dev_b)
        tok_arrived(unit_a)
        pass_on(tok.at[unit_a], unit_a, s2_send.at[k, 1], dev_b)
        pass_on(tok.at[unit_a], unit_a, s3_send.at[k, 1], dev_s)

    def f3(k):
        for at, jj in ((2, jb), (3, jab)):
            unit = plane(k) * SPLIT + jj
            tok_arrived(unit)
            pass_on(tok.at[unit], unit, s3_send.at[k, at], dev_s)

    k_tile = tile_of(width, 1792)
    n_tile = tile_of(width, 1024)

    def compute(k):
        first = plane(k) * SPLIT
        if k == 0:
            for load in loads:
                load.wait()
        for q in range(QUADS):
            tok_arrived(first + 2 * q + (1 - c))

        def up_step(t, acc):
            cols = pl.ds(pl.multiple_of(t * k_tile, k_tile), k_tile)
            xs = tok[pl.ds(first, SPLIT), :, cols]
            xs = xs.astype(jnp.float32).reshape(SPLIT * rows, k_tile).astype(jnp.bfloat16)
            g, u = acc
            g = g + jnp.dot(xs, gate_w[cols, :], preferred_element_type=jnp.float32)
            u = u + jnp.dot(xs, up_w[cols, :], preferred_element_type=jnp.float32)
            return g, u

        zero = jnp.zeros((SPLIT * rows, hid), jnp.float32)
        g, u = lax.fori_loop(0, width // k_tile, up_step, (zero, zero))
        hidden = (jax.nn.silu(g) * u).astype(jnp.bfloat16)

        def down_step(t, carry):
            cols = pl.ds(pl.multiple_of(t * n_tile, n_tile), n_tile)
            d = jnp.dot(hidden, down_w[:, cols], preferred_element_type=jnp.float32)
            part[pl.ds(first, SPLIT), :, cols] = d.reshape(SPLIT, rows, n_tile).astype(jnp.bfloat16)
            return carry

        lax.fori_loop(0, width // n_tile, down_step, 0)
        for q in range(QUADS):
            send(part.at[first + 2 * q + (1 - c)], rb3.at[k, q],
                 r3_send.at[k, q], r3_recv.at[k, q], dev_s)

    f32 = jnp.float32

    def r2(k):
        for at, jj in ((1, jab), (0, jb)):
            unit, q = plane(k) * SPLIT + jj, jj // 2
            arrived(rb3.at[k, q], r3_recv.at[k, q])
            part[unit] = (part[unit].astype(f32) + rb3[k, q].astype(f32)).astype(jnp.bfloat16)
            send(part.at[unit], rb2.at[k, at], r2_send.at[k, at], r2_recv.at[k, at], dev_b)

    def r1(k):
        unit, q = plane(k) * SPLIT + ja, ja // 2
        arrived(rb3.at[k, q], r3_recv.at[k, q])
        arrived(rb2.at[k, 1], r2_recv.at[k, 1])
        part[unit] = (
            part[unit].astype(f32) + rb3[k, q].astype(f32) + rb2[k, 1].astype(f32)
        ).astype(jnp.bfloat16)
        send(part.at[unit], rb1.at[k], r1_send.at[k], r1_recv.at[k], dev_a)

    def r0(k):
        unit, q = plane(k) * SPLIT + j, j // 2
        arrived(rb3.at[k, q], r3_recv.at[k, q])
        arrived(rb2.at[k, 0], r2_recv.at[k, 0])
        arrived(rb1.at[k], r1_recv.at[k])
        part[unit] = (
            (part[unit].astype(f32) + rb3[k, q].astype(f32))
            + (rb2[k, 0].astype(f32) + rb1[k].astype(f32))
        ).astype(jnp.bfloat16)
        if k > 0:
            send(part.at[unit], rb0.at[k], r0_send.at[k], r0_recv.at[k], unit)

    for k in range(1, E):
        pass_on(tok_hbm, me, z_send.at[k], ((z + E - k) % E) * SPLIT + j)
    f1(0)
    for i in range(E + 3):
        steps = ((f2, i), (f1, i + 1), (r2, i - 2), (compute, i - 1), (f3, i), (r1, i - 2), (r0, i - 3))
        for step, k in steps:
            if 0 <= k < E:
                step(k)

    affinity = aff_ref[...]
    weight = route_scale * affinity / jnp.sum(affinity, axis=1, keepdims=True)
    ids = ids_ref[...]

    def weighted(values, expert):
        w = jnp.sum(jnp.where(ids == expert, weight, 0.0), axis=1, keepdims=True)
        return w * values.astype(f32)

    total = weighted(part[me], z)
    for k in range(1, E):
        arrived(rb0.at[k], r0_recv.at[k])
        total = total + weighted(rb0[k], (z + E - k) % E)
    out_ref[...] = total.astype(out_ref.dtype)
    for copy in sends:
        copy.wait_send()


def body(tokens, expert_ids, affinity, w_gate, w_up, w_down):
    n = lax.axis_size("ep")
    experts = n // SPLIT
    rows, width = tokens.shape
    hid = w_gate.shape[2]
    dma = pltpu.SemaphoreType.DMA
    bf16 = jnp.bfloat16
    unit = (rows, width)
    hbm = pl.BlockSpec(memory_space=pltpu.MemorySpace.HBM)
    vmem = pl.BlockSpec(memory_space=pltpu.MemorySpace.VMEM)
    return pl.pallas_call(
        functools.partial(kernel, experts),
        out_shape=jax.ShapeDtypeStruct(unit, bf16),
        in_specs=[hbm, vmem, vmem, hbm, hbm, hbm],
        out_specs=vmem,
        scratch_shapes=[
            pltpu.VMEM((n,) + unit, bf16),
            pltpu.VMEM((n,) + unit, bf16),
            pltpu.VMEM((experts, QUADS) + unit, bf16),
            pltpu.VMEM((experts, 2) + unit, bf16),
            pltpu.VMEM((experts,) + unit, bf16),
            pltpu.VMEM((experts,) + unit, bf16),
            pltpu.VMEM((width, hid), bf16),
            pltpu.VMEM((width, hid), bf16),
            pltpu.VMEM((hid, width), bf16),
            dma,
            dma((3,)),
            dma((n,)),
            dma((experts,)),
            dma((experts,)),
            dma((experts, 2)),
            dma((experts, QUADS)),
            dma((experts, QUADS)),
            dma((experts, QUADS)),
            dma((experts, 2)),
            dma((experts, 2)),
            dma((experts,)),
            dma((experts,)),
            dma((experts,)),
            dma((experts,)),
        ],
        compiler_params=pltpu.CompilerParams(
            collective_id=0, has_side_effects=True, vmem_limit_bytes=VMEM_LIMIT
        ),
    )(tokens, expert_ids, affinity, w_gate, w_up, w_down)


def solution(mesh):
    return jax.shard_map(
        body,
        mesh=mesh,
        in_specs=(
            P(("groups", "ep"), None),
            P(("groups", "ep"), None),
            P(("groups", "ep"), None),
            P("ep", None, None),
            P("ep", None, None),
            P("ep", None, None),
        ),
        out_specs=P(("groups", "ep"), None),
        check_vma=False,
    )
```

time: 195 us -> 59.7 us (0.31)
  blocking collectives: 176 us -> 0 us
  Pallas kernels: 0 us -> 55.2 us
  matrix products: 12.7 us -> 0 us
  other arithmetic: 2.36 us -> 0 us
    all_to_all x2 -> x0, blocking collectives: 176 us -> none  [the longest x1 90.2 us: body(): lax.all_to_all(outgoing, 'ep', split_axis=0, concat_axis=0, tiled=True)]
    pallas_call x0 -> x1, Pallas kernels: none -> 55.2 us  [body(): pl.pallas_call(functools.partial(kernel, experts), out_shape=jax.ShapeDty...]
    dot_general x4 -> x0, matrix products: 12.7 us -> none  [the longest x1 10 us: body(): jnp.dot(hidden, w_down[0], preferred_element_type=jnp.float32)]
    unnamed x7 -> x3, local copies, waits for them, and re-layouts: 2.56 us -> 4.24 us
where the time goes in v1:
time: 59.7 us; the launch traced here: 59.4 us
  Pallas kernels  55.2 us (92%)
  local copies, waits for them, and re-layouts  4.24 us (7%)
    pallas_call x1, Pallas kernels, body(): pl.pallas_call(functools.partial(kernel, experts), out_shape=jax.ShapeDty...  55.2 us
    unnamed x3, local copies, waits for them, and re-layouts  4.24 us

profile of v1, /device:TPU:0, one launch (start us, length us, event | category | flops | bytes accessed | tf_op | source)
XLA Modules:
  0.0 59.4 jit_solution(5730886409719773520)
XLA Ops:
  0.0 1.3 %copy.7.ids_ref = s32[8,2]{1,0:T(8,128)} copy(s32[8,2]{0,1:T(2,128)} %param.7) | data formatting | bytes 128 | tf_op args[1]
  1.3 1.3 %copy.8.aff_ref = f32[8,2]{1,0:T(8,128)} copy(f32[8,2]{0,1:T(2,128)} %param.8) | data formatting | bytes 128 | tf_op args[2]
  2.7 55.2 %shard_map.64 = bf16[8,7168]{1,0:T(8,128)(2,1)} custom-call(bf16[8,7168]{1,0:T(8,128)(2,1)} %tok_hbm.1, s32[8,2]{1,0:T(8,128)} %copy.7.ids_ref, f32[8,2]{1,0:T(8,128)} %copy.8.aff_ref, bf16[1,7168,256]{2,1,0:T(8,128)(2,1)} %gate_hbm.1, bf16[1,7168,256]{2,1,0:T(8,128)(2,1)} %up_hbm.1, bf16[1,256,7168]{2,1,0:T(8,128)(2,1)} %down_hbm.1), custom_call_target="tpu_custom_call" | custom-call | tf_op jit(solution)/shard_map/pallas_call | solution.py:217
  57.9 1.6 %copy.10 = bf16[8,7168]{1,0:T(8,128)(2,1)} copy(bf16[8,7168]{1,0:T(8,128)(2,1)} %shard_map.64) | data formatting | bytes 229376

commit v2 on v1

--- a/solution.py
+++ b/solution.py
@@ -24,9 +24,16 @@
     return best
 
 
+def shifts(experts):
+    shift = [0]
+    for step in range(1, experts // 2 + 1):
+        shift += [step] if 2 * step == experts else [step, experts - step]
+    return shift
+
+
 def kernel(
     experts,
-    tok_hbm, ids_ref, aff_ref, gate_hbm, up_hbm, down_hbm,
+    tok_hbm, gate_hbm, up_hbm, down_hbm,
     out_ref,
     tok, part, rb3, rb2, rb1, rb0, gate_w, up_w, down_w,
     load_sem, w_sem, tok_recv, z_send, s1_send, s2_send, s3_send,
@@ -50,8 +57,13 @@
     base = z * SPLIT
     dev_a, dev_b, dev_s = base + ja, base + jb, base + js
 
+    shift = shifts(E)
+
     def plane(k):
-        return (z + k) % E
+        return (z + shift[k]) % E
+
+    def plane_back(k):
+        return (z + E - shift[k]) % E
 
     loads = [
         pltpu.make_async_copy(tok_hbm, tok.at[me], load_sem),
@@ -98,31 +110,36 @@
         if k > 0:
             tok_arrived(unit)
         pass_on(own(k), unit, s1_send.at[k], dev_a)
+        pass_on(own(k), unit, s2_send.at[k, 0], dev_b)
         pass_on(own(k), unit, s3_send.at[k, 0], dev_s)
 
     def f2(k):
-        unit, unit_a = plane(k) * SPLIT + j, plane(k) * SPLIT + ja
-        pass_on(own(k), unit, s2_send.at[k, 0], dev_b)
+        unit_a = plane(k) * SPLIT + ja
         tok_arrived(unit_a)
         pass_on(tok.at[unit_a], unit_a, s2_send.at[k, 1], dev_b)
         pass_on(tok.at[unit_a], unit_a, s3_send.at[k, 1], dev_s)
 
-    def f3(k):
-        for at, jj in ((2, jb), (3, jab)):
-            unit = plane(k) * SPLIT + jj
-            tok_arrived(unit)
-            pass_on(tok.at[unit], unit, s3_send.at[k, at], dev_s)
+    def f3(k, at=2, jj=jb):
+        unit = plane(k) * SPLIT + jj
+        tok_arrived(unit)
+        pass_on(tok.at[unit], unit, s3_send.at[k, at], dev_s)
+
+    def f4(k):
+        f3(k, 3, jab)
 
     k_tile = tile_of(width, 1792)
     n_tile = tile_of(width, 1024)
 
-    def compute(k):
+    held = {}
+
+    def up(k, half):
         first = plane(k) * SPLIT
-        if k == 0:
+        if k == 0 and half == 0:
             for load in loads:
                 load.wait()
-        for q in range(QUADS):
-            tok_arrived(first + 2 * q + (1 - c))
+        if half == 0:
+            for q in range(QUADS):
+                tok_arrived(first + 2 * q + (1 - c))
 
         def up_step(t, acc):
             cols = pl.ds(pl.multiple_of(t * k_tile, k_tile), k_tile)
@@ -134,8 +151,16 @@
             return g, u
 
         zero = jnp.zeros((SPLIT * rows, hid), jnp.float32)
-        g, u = lax.fori_loop(0, width // k_tile, up_step, (zero, zero))
-        hidden = (jax.nn.silu(g) * u).astype(jnp.bfloat16)
+        count = width // k_tile
+        if half == 0:
+            held[k] = lax.fori_loop(0, count // 2, up_step, (zero, zero))
+        else:
+            g, u = lax.fori_loop(count // 2, count, up_step, held[k])
+            held[k] = (jax.nn.silu(g) * u).astype(jnp.bfloat16)
+
+    def down(k):
+        first = plane(k) * SPLIT
+        hidden = held.pop(k)
 
         def down_step(t, carry):
             cols = pl.ds(pl.multiple_of(t * n_tile, n_tile), n_tile)
@@ -150,12 +175,14 @@
 
     f32 = jnp.float32
 
-    def r2(k):
-        for at, jj in ((1, jab), (0, jb)):
-            unit, q = plane(k) * SPLIT + jj, jj // 2
-            arrived(rb3.at[k, q], r3_recv.at[k, q])
-            part[unit] = (part[unit].astype(f32) + rb3[k, q].astype(f32)).astype(jnp.bfloat16)
-            send(part.at[unit], rb2.at[k, at], r2_send.at[k, at], r2_recv.at[k, at], dev_b)
+    def ra(k, at=1, jj=jab):
+        unit, q = plane(k) * SPLIT + jj, jj // 2
+        arrived(rb3.at[k, q], r3_recv.at[k, q])
+        part[unit] = (part[unit].astype(f32) + rb3[k, q].astype(f32)).astype(jnp.bfloat16)
+        send(part.at[unit], rb2.at[k, at], r2_send.at[k, at], r2_recv.at[k, at], dev_b)
+
+    def rb(k):
+        ra(k, 0, jb)
 
     def r1(k):
         unit, q = plane(k) * SPLIT + ja, ja // 2
@@ -179,27 +206,23 @@
             send(part.at[unit], rb0.at[k], r0_send.at[k], r0_recv.at[k], unit)
 
     for k in range(1, E):
-        pass_on(tok_hbm, me, z_send.at[k], ((z + E - k) % E) * SPLIT + j)
-    f1(0)
-    for i in range(E + 3):
-        steps = ((f2, i), (f1, i + 1), (r2, i - 2), (compute, i - 1), (f3, i), (r1, i - 2), (r0, i - 3))
-        for step, k in steps:
+        pass_on(tok_hbm, me, z_send.at[k], plane_back(k) * SPLIT + j)
+    steps = {
+        "f1": f1, "f2": f2, "f3": f3, "f4": f4,
+        "up0": lambda k: up(k, 0), "up1": lambda k: up(k, 1), "down": down,
+        "ra": ra, "rb": rb, "r1": r1, "r0": r0,
+    }
+    for i in range(-1, E + 5):
+        for name, k in (
+            ("f2", i + 0), ("f1", i + 1), ("ra", i + -2), ("rb", i + -2), ("up0", i + -1), ("up1", i + -1), ("down", i + -1), ("f3", i + 0), ("f4", i + 0), ("r1", i + -2), ("r0", i + -3),
+        ):
             if 0 <= k < E:
-                step(k)
-
-    affinity = aff_ref[...]
-    weight = route_scale * affinity / jnp.sum(affinity, axis=1, keepdims=True)
-    ids = ids_ref[...]
-
-    def weighted(values, expert):
-        w = jnp.sum(jnp.where(ids == expert, weight, 0.0), axis=1, keepdims=True)
-        return w * values.astype(f32)
-
-    total = weighted(part[me], z)
+                steps[name](k)
+
+    out_ref[0] = part[me]
     for k in range(1, E):
         arrived(rb0.at[k], r0_recv.at[k])
-        total = total + weighted(rb0[k], (z + E - k) % E)
-    out_ref[...] = total.astype(out_ref.dtype)
+        out_ref[k] = rb0[k]
     for copy in sends:
         copy.wait_send()
 
@@ -214,10 +237,10 @@
     unit = (rows, width)
     hbm = pl.BlockSpec(memory_space=pltpu.MemorySpace.HBM)
     vmem = pl.BlockSpec(memory_space=pltpu.MemorySpace.VMEM)
-    return pl.pallas_call(
+    sums = pl.pallas_call(
         functools.partial(kernel, experts),
-        out_shape=jax.ShapeDtypeStruct(unit, bf16),
-        in_specs=[hbm, vmem, vmem, hbm, hbm, hbm],
+        out_shape=jax.ShapeDtypeStruct((experts,) + unit, bf16),
+        in_specs=[hbm, hbm, hbm, hbm],
         out_specs=vmem,
         scratch_shapes=[
             pltpu.VMEM((n,) + unit, bf16),
@@ -248,7 +271,18 @@
         compiler_params=pltpu.CompilerParams(
             collective_id=0, has_side_effects=True, vmem_limit_bytes=VMEM_LIMIT
         ),
-    )(tokens, expert_ids, affinity, w_gate, w_up, w_down)
+    )(tokens, w_gate, w_up, w_down)
+    routes = expert_ids.shape[1]
+    share = route_scale * affinity / jnp.sum(affinity, axis=1, keepdims=True)
+    z = lax.axis_index("ep") // SPLIT
+    total = jnp.zeros(unit, jnp.float32)
+    for k, step in enumerate(shifts(experts)):
+        expert = (z + experts - step) % experts
+        weight = sum(
+            jnp.where(expert_ids[:, r] == expert, share[:, r], 0.0) for r in range(routes)
+        )
+        total = total + weight[:, None] * sums[k].astype(jnp.float32)
+    return total.astype(bf16)
 
 
 def solution(mesh):

time: 59.7 us -> 58.2 us (0.975)
  other arithmetic: 0 us -> 4.77 us
  local copies, waits for them, and re-layouts: 4.24 us -> 0 us
  Pallas kernels: 55.2 us -> 52.9 us
    unnamed x3 -> x0, local copies, waits for them, and re-layouts: 4.24 us -> none
    pallas_call x1, Pallas kernels: 55.2 us -> 52.9 us  [body(): pl.pallas_call(functools.partial(kernel, experts), out_shape=jax.ShapeDty...]
    convert_element_type x0 -> x1, other arithmetic: none -> 1.87 us  [body(): return total.astype(bf16)]
    mul x0 -> x2, other arithmetic: none -> 1.52 us  [body(): total = total + weight[:, None] * sums[k].astype(jnp.float32)]
    reduce_sum x0 -> x1, other arithmetic: none -> 0.7 us  [body(): share = route_scale * affinity / jnp.sum(affinity, axis=1, keepdims=True)]
    div x0 -> x1, other arithmetic: none -> 0.68 us  [body(): share = route_scale * affinity / jnp.sum(affinity, axis=1, keepdims=True)]
where the time goes in v2:
time: 58.2 us; the launch traced here: 57.7 us
  Pallas kernels  52.9 us (91%)
  other arithmetic  4.77 us (8%)
    pallas_call x1, Pallas kernels, body(): pl.pallas_call(functools.partial(kernel, experts), out_shape=jax.ShapeDty...  52.9 us
    convert_element_type x1, other arithmetic, body(): return total.astype(bf16)  1.87 us
    mul x2, other arithmetic, body(): total = total + weight[:, None] * sums[k].astype(jnp.float32)  1.52 us

profile of v2, /device:TPU:0, one launch (start us, length us, event | category | flops | bytes accessed | tf_op | source)
XLA Modules:
  0.0 57.7 jit_solution(18136546784734524267)
XLA Ops:
  0.0 0.7 %reduce_sum.9 = f32[8]{0:T(128)S(1)} reduce(f32[8,2]{0,1:T(2,128)} %param.8, f32[]{:T(128)} %constant.55.clone.1), dimensions={1}, to_apply=%region_0.0 | reduce | flops 8 | bytes 100 | tf_op jit(solution)/shard_map/reduce_sum | solution.py:276
  0.7 0.7 %multiply_divide_fusion = f32[8,2]{0,1:T(2,128)S(1)} fusion(f32[8,2]{0,1:T(2,128)} %param.8, f32[8]{0:T(128)S(1)} %reduce_sum.9), kind=kLoop, calls=%fused_computation.16 | loop fusion | flops 32 | bytes 160 | tf_op jit(solution)/shard_map/div | solution.py:276
  1.4 0.8 %fusion.10 = f32[8]{0:T(128)S(1)} fusion(s32[]{:T(128)S(6)} %select_n.60, f32[8,2]{0,1:T(2,128)S(1)} %multiply_divide_fusion, s32[8,2]{0,1:T(2,128)} %param.7), kind=kLoop, calls=%fused_computation.23 | loop fusion | flops 40 | bytes 164 | tf_op jit(solution)/shard_map/mul | solution.py:284
  2.1 0.8 %fusion.11 = (f32[8]{0:T(128)S(1)}, f32[8]{0:T(128)S(1)}, f32[8]{0:T(128)S(1)}) fusion(s32[]{:T(128)S(6)} %select_n.57, f32[8,2]{0,1:T(2,128)S(1)} %multiply_divide_fusion, s32[8,2]{0,1:T(2,128)} %param.7, s32[]{:T(128)S(6)} %select_n.63, s32[]{:T(128)S(6)} %select_n.66), kind=kLoop, calls=%fused_computation.24 | loop fusion | flops 120 | bytes 236 | tf_op jit(solution)/shard_map/mul | solution.py:284
  2.9 52.9 %shard_map.64 = bf16[4,8,7168]{2,1,0:T(8,128)(2,1)} custom-call(bf16[8,7168]{1,0:T(8,128)(2,1)} %tok_hbm.1, bf16[1,7168,256]{2,1,0:T(8,128)(2,1)} %gate_hbm.1, bf16[1,7168,256]{2,1,0:T(8,128)(2,1)} %up_hbm.1, bf16[1,256,7168]{2,1,0:T(8,128)(2,1)} %down_hbm.1), custom_call_target="tpu_custom_call" | custom-call | tf_op jit(solution)/shard_map/pallas_call | solution.py:240
  55.8 1.9 %fusion.1 = bf16[8,7168]{1,0:T(8,128)(2,1)} fusion(bf16[4,8,7168]{2,1,0:T(8,128)(2,1)} %shard_map.64, f32[8]{0:T(128)S(1)} %get-tuple-element.7, f32[8]{0:T(128)S(1)} %get-tuple-element.6, f32[8]{0:T(128)S(1)} %fusion.10, f32[8]{0:T(128)S(1)} %get-tuple-element.5), kind=kLoop, calls=%fused_computation.2 | loop fusion | flops 688128 | bytes 573568 | tf_op jit(solution)/shard_map/convert_element_type | solution.py:285

commit v3 on v2

--- a/solution.py
+++ b/solution.py
@@ -273,15 +273,18 @@
         ),
     )(tokens, w_gate, w_up, w_down)
     routes = expert_ids.shape[1]
-    share = route_scale * affinity / jnp.sum(affinity, axis=1, keepdims=True)
     z = lax.axis_index("ep") // SPLIT
-    total = jnp.zeros(unit, jnp.float32)
-    for k, step in enumerate(shifts(experts)):
-        expert = (z + experts - step) % experts
-        weight = sum(
-            jnp.where(expert_ids[:, r] == expert, share[:, r], 0.0) for r in range(routes)
+    total_affinity = sum(affinity[:, r : r + 1] for r in range(routes))
+    expert = (z + experts - jnp.array(shifts(experts), jnp.int32)[None, :]) % experts
+    weight = sum(
+        jnp.where(
+            expert_ids[:, r : r + 1] == expert,
+            route_scale * affinity[:, r : r + 1] / total_affinity,
+            0.0,
         )
-        total = total + weight[:, None] * sums[k].astype(jnp.float32)
+        for r in range(routes)
+    )
+    total = sum(weight[:, k : k + 1] * sums[k].astype(jnp.float32) for k in range(experts))
     return total.astype(bf16)
 
 

time: 58.2 us -> 57.6 us (0.990)
  other arithmetic: 4.77 us -> 3.36 us
  local copies, waits for them, and re-layouts: 0 us -> 0.76 us
    mul x2 -> x0, other arithmetic: 1.52 us -> none  [body(): total = total + weight[:, None] * sums[k].astype(jnp.float32)]
    broadcast_in_dim x0 -> x1, other arithmetic: none -> 0.76 us  [body(): jnp.where(expert_ids[:, r:r + 1] == expert, route_scale * affinity[:, r:r...]
    eq x0 -> x1, local copies, waits for them, and re-layouts: none -> 0.76 us  [body(): expert_ids[:, r:r + 1] == expert]
    reduce_sum x1 -> x0, other arithmetic: 0.7 us -> none  [body(): share = route_scale * affinity / jnp.sum(affinity, axis=1, keepdims=True)]
    div x1 -> x0, other arithmetic: 0.68 us -> none  [body(): share = route_scale * affinity / jnp.sum(affinity, axis=1, keepdims=True)]
    select_n x0 -> x1, other arithmetic: none -> 0.66 us  [body(): (z + experts - jnp.array(shifts(experts), jnp.int32)[None, :]) % experts]
where the time goes in v3:
time: 57.6 us; the launch traced here: 57 us
  Pallas kernels  52.9 us (92%)
  other arithmetic  3.36 us (6%)
  local copies, waits for them, and re-layouts  0.76 us (1%)
    pallas_call x1, Pallas kernels, body(): pl.pallas_call(functools.partial(kernel, experts), out_shape=jax.ShapeDty...  52.9 us
    convert_element_type x1, other arithmetic, body(): return total.astype(bf16)  1.87 us

profile of v3, /device:TPU:0, one launch (start us, length us, event | category | flops | bytes accessed | tf_op | source)
XLA Modules:
  0.0 57.0 jit_solution(7346179608965983939)
XLA Ops:
  0.0 0.7 %and_select_fusion = s32[4]{0:T(128)S(1)} fusion(s32[4]{0:T(128)} %constant.46, s32[]{:T(128)S(6)} %add.26), kind=kLoop, calls=%fused_computation.11 | loop fusion | flops 48 | bytes 36 | tf_op jit(solution)/shard_map/jit(remainder)/select_n | solution.py:278
  0.7 0.8 %slice_bitcast_fusion.5 = (s32[8]{0:T(128)S(1)}, s32[8]{0:T(128)S(1)}) fusion(s32[8,2]{0,1:T(2,128)} %param.8), kind=kLoop, calls=%fused_computation.20 | loop fusion | bytes 128 | tf_op jit(solution)/shard_map/eq | solution.py:281
  1.4 0.8 %fusion.5 = (f32[8]{0:T(128)S(1)}, f32[8]{0:T(128)S(1)}) fusion(f32[8,2]{0,1:T(2,128)} %param.9), kind=kLoop, calls=%fused_computation.21 | loop fusion | flops 40 | bytes 128 | tf_op jit(solution)/shard_map/jit(_where)/broadcast_in_dim | solution.py:280
  2.2 0.1 select_add_fusion
  2.3 52.9 %shard_map.73 = bf16[4,8,7168]{2,1,0:T(8,128)(2,1)} custom-call(bf16[8,7168]{1,0:T(8,128)(2,1)} %tok_hbm.1, bf16[1,7168,256]{2,1,0:T(8,128)(2,1)} %gate_hbm.1, bf16[1,7168,256]{2,1,0:T(8,128)(2,1)} %up_hbm.1, bf16[1,256,7168]{2,1,0:T(8,128)(2,1)} %down_hbm.1), custom_call_target="tpu_custom_call" | custom-call | tf_op jit(solution)/shard_map/pallas_call | solution.py:240
  55.2 1.9 %fusion.1 = bf16[8,7168]{1,0:T(8,128)(2,1)} fusion(bf16[4,8,7168]{2,1,0:T(8,128)(2,1)} %shard_map.73, f32[8]{0:T(128)S(1)} %get-tuple-element.6, f32[8]{0:T(128)S(1)} %get-tuple-element.7, f32[8]{0:T(128)S(1)} %get-tuple-element.8, f32[8]{0:T(128)S(1)} %get-tuple-element.5), kind=kLoop, calls=%fused_computation.2 | loop fusion | flops 688128 | bytes 573568 | tf_op jit(solution)/shard_map/convert_element_type | solution.py:288
  (1 shorter events, 0.0 us)
